TPU v7x, 256 devices: a whole 4x4x8 slice. The times are simulated.
256 devices in a mesh: ctx: 32 (over x, z), grp: 8 (over y, core).
Axes of the slice: x: 4, y: 4, z: 8, core: 2. Of those that a mesh axis runs over, the one named last changes fastest.
Arguments:
- out_grad: bfloat16 [16384, 2048], P('ctx', 'grp'), may hold values from -6 to 6
- filter_mats: bfloat16 [16, 2048, 2048], P('grp', 'ctx'), may hold values from -0.125 to 0.125
- coeffs: float32 [16, 80], replicated, may hold values from -0.15625 to 0.15625
- pole_rates: float32 [80], replicated, may hold values from 1.2207031e-06 to 0.03
Outputs:
- in_grad: bfloat16 [16384, 2048], P('ctx', 'grp')
All inputs are finite; a program needn't handle non-finite values.
Results may differ from a plain program's by a relative error of at most 0.001.
Values may be sent and summed in bfloat16 or wider, within the bound.
A program may use at most 128 MiB of HBM per device.

v0:
```python
import jax
import jax.numpy as jnp
from jax import lax
from jax.sharding import PartitionSpec as P

exact_prec = lax.Precision.HIGHEST


def entering(array, axis, combine, identity):
    count, here = (lax.axis_size(axis), lax.axis_index(axis))
    everything = jax.tree.map(lambda part: lax.all_gather(part, axis), array)
    start = jax.tree.map(
        lambda part, zero: jnp.broadcast_to(jnp.asarray(zero, part.dtype), part.shape),
        array,
        identity,
    )

    def step(k, before):
        at = count - 1 - k
        reached = at > here
        new = combine(before, jax.tree.map(lambda part: part[at], everything))
        return jax.tree.map(lambda a, b: jnp.where(reached, a, b), new, before)

    return lax.fori_loop(0, count, step, start)


def merge_suffix(earlier, latter):
    carried_e, factor_e = earlier
    carried_l, factor_l = latter
    return (carried_l + factor_l * carried_e, factor_l * factor_e)


def per_device(out_grad, filter_mats, coeffs, pole_rates):
    full_grad = lax.all_gather(out_grad, "grp", axis=1, tiled=True)
    length = full_grad.shape[0]
    col_width = out_grad.shape[1]
    poles = pole_rates.shape[0]
    positions = jnp.arange(length, dtype=jnp.float32)
    pole_gains = jnp.sqrt(-jnp.expm1(-2.0 * pole_rates))
    middle = float(length // 2)
    rising = jnp.exp(-(positions[:, None] - middle) * pole_rates[None, :])
    falling = jnp.exp((positions[:, None] - middle) * pole_rates[None, :])
    causal = positions[:, None] >= positions[None, :]
    decay_pos = jnp.exp(-positions[:, None] * pole_rates[None, :])
    edge_decay = pole_gains[None, :] * jnp.exp(-(length - positions)[:, None] * pole_rates[None, :])
    block_decay = jnp.exp(-length * pole_rates)[:, None]
    unit_factor = jnp.ones((poles, 1), jnp.float32)
    filters = filter_mats.shape[0]
    own_coeffs = lax.dynamic_slice_in_dim(coeffs, lax.axis_index("grp") * filters, filters, 0)
    kernel_mat = jnp.einsum(
        "tp,kp,sp->kts", rising, own_coeffs * pole_gains[None, :], falling, precision=exact_prec
    )
    kernel_mat = jnp.where(causal[None], kernel_mat, 0.0)
    weights = own_coeffs[:, :, None] * decay_pos.T[None]
    proj_grad = jnp.einsum(
        "tj,kij->kti",
        full_grad,
        lax.all_gather(filter_mats, "ctx", axis=1, tiled=True),
        preferred_element_type=jnp.float32,
    )
    near_part = jnp.einsum("kts,kti->si", kernel_mat, proj_grad, precision=exact_prec)
    pole_part = jnp.einsum("kpt,kti->pi", weights, proj_grad, precision=exact_prec)
    stacked = jnp.concatenate([near_part, pole_part], axis=0)
    near_sum = lax.psum_scatter(stacked[:length], "grp", scatter_dimension=1, tiled=True)
    pole_sum = lax.psum(stacked[length:], "grp")
    later_all = entering(
        (pole_sum, block_decay), "ctx", merge_suffix, (jnp.zeros_like(pole_sum), unit_factor)
    )[0]
    own_cols = lax.dynamic_slice_in_dim(later_all, lax.axis_index("grp") * col_width, col_width, 1)
    total = near_sum + jnp.dot(edge_decay, own_cols, precision=exact_prec)
    return total.astype(jnp.bfloat16)


def solution(mesh):
    placed = (P("ctx", "grp"), P("grp", "ctx", None), P(), P())
    return jax.shard_map(
        per_device, mesh=mesh, in_specs=placed, out_specs=P("ctx", "grp"), check_vma=False
    )
```

profile of v0, /device:TPU:0, one launch (start us, length us, event | category | flops | bytes accessed | tf_op | source)
XLA Modules:
  0.0 490.5 jit_solution(5679977234924721466)
XLA Ops:
  8.1 1.3 dynamic-slice
  12.2 27.7 %all-gather.7.cloned.1.call-done = bf16[512,2048]{1,0:T(8,128)(2,1)} async-done(((bf16[512,256]{1,0:T(8,128)(2,1)}), bf16[512,2048]{1,0:T(8,128)(2,1)}) %all-gather.7.cloned.1.call-update) | async-done | bytes 2097168 | tf_op jit(solution)/shard_map/all_gather | solution.py:34
  39.9 143.1 %all-gather.5.cloned.1.call-done = bf16[2,2048,2048]{2,1,0:T(8,128)(2,1)} async-done(((bf16[2,64,2048]{2,1,0:T(8,128)(2,1)}), bf16[2,2048,2048]{2,1,0:T(8,128)(2,1)}) %all-gather.5.cloned.1.call-update) | async-done | bytes 16777232 | tf_op jit(solution)/shard_map/all_gather | solution.py:58
  183.0 12.9 %fusion.11 = f32[2,2048,512]{2,1,0:T(8,128)S(1)} fusion(bf16[2,2048,2048]{2,1,0:T(8,128)(2,1)} %all-gather.5.cloned.1.call-done, bf16[512,2048]{1,0:T(8,128)(2,1)} %all-gather.7.cloned.1.call-done), kind=kOutput, calls=%fused_computation.9 | convolution fusion | flops 8589934592 | bytes 27262976 | tf_op jit(solution)/shard_map/tj,kij->kti/dot_general | solution.py:55
  195.9 3.3 copy-done
  199.2 9.1 %fusion.8 = f32[1,80,2048]{2,1,0:T(8,128)} fusion(f32[2,2048,512]{2,1,0:T(8,128)S(1)} %fusion.11, f32[80,512]{1,0:T(8,128)S(1)} %multiply_exponential_fusion, f32[2,80]{1,0:T(2,128)S(1)} %get-tuple-element.167), kind=kOutput, calls=%fused_computation.8 | convolution fusion | flops 2013347840 | bytes 9208448 | tf_op jit(solution)/shard_map/kpt,kti->pi/dot_general | solution.py:62
  208.3 63.9 %all-reduce.3.cloned.1.call-done = f32[1,80,2048]{2,1,0:T(8,128)} async-done(((f32[1,80,2048]{2,1,0:T(8,128)}), f32[1,80,2048]{2,1,0:T(8,128)}) %all-reduce.3.cloned.1.call-update) | async-done | bytes 655376 | tf_op jit(solution)/shard_map/psum | solution.py:65
  272.4 147.7 %all-reduce = f32[2560]{0:T(1024)S(1)} all-reduce(f32[2560]{0:T(1024)S(1)} %get-tuple-element.168), channel_id=2, replica_groups=mesh['ctx'=32,'grp'=8] {'ctx'}, use_global_device_ids=true, to_apply=%add | all-reduce | flops 2560 | bytes 20480
  420.7 1.9 fusion.17
  422.6 17.5 %fusion.5 = f32[512,2048]{1,0:T(8,128)} fusion(f32[2,2048,512]{2,1,0:T(8,128)} %copy-done, f32[2,512,512]{1,2,0:T(8,128)S(1)} %fusion.17, pred[512,512]{0,1:T(8,128)(4,1)S(1)} %iota_compare_fusion), kind=kOutput, calls=%fused_computation.7 | convolution fusion | flops 12885426176 | bytes 14942208 | tf_op jit(solution)/shard_map/kts,kti->si/dot_general | solution.py:61
  440.1 41.4 %while.16 = (s32[]{:T(128)}, f32[80,2048]{1,0:T(8,128)S(1)}, s32[]{:T(128)}, f32[32,80,2048]{2,1,0:T(8,128)}, f32[32,80,1]{1,2,0:T(1,128)S(1)}, /*index=5*/s32[]{:T(128)}, s32[]{:T(128)}, s32[]{:T(128)}, s32[]{:T(128)}) while((s32[]{:T(128)}, f32[80,2048]{1,0:T(8,128)S(1)}, s32[]{:T(128)}, f32[32,80,2048]{2,1,0:T(8,128)}, ...), condition=%wide.region_3.4_spmd.clone, body=%wide.region_2.3_spmd.clone.sunk | while | flops 655368 | bytes 1967215 | solution.py:24
  445.3 1.2 fusion.39
  446.6 1.3 fusion.39
  450.5 1.2 fusion.39
  451.8 1.3 fusion.39
  453.1 1.2 fusion.39
  454.4 1.2 fusion.39
  455.7 1.2 fusion.39
  458.3 1.2 fusion.39
  459.6 1.2 fusion.39
  460.8 1.2 fusion.39
  462.1 1.3 fusion.39
  463.4 1.2 fusion.39
  466.0 1.3 fusion.39
  467.3 1.3 fusion.39
  468.6 1.2 fusion.39
  469.9 1.2 fusion.39
  472.5 1.2 fusion.39
  473.8 1.2 fusion.39
  475.1 1.2 fusion.39
  479.0 1.2 fusion.39
  481.5 2.5 fusion.14
  (73 shorter events, 19.7 us)
Async XLA Ops:
  6.5 33.4 %all-gather.7.cloned.1.call-start = ((), (), s32[]{:S(2)}) async-start(), calls=%async_computation.2 | async-start | bytes 2359296 | tf_op jit(solution)/shard_map/all_gather | solution.py:34
  7.3 175.8 %all-gather.5.cloned.1.call-start = ((), (), s32[]{:S(2)}) async-start(), calls=%async_computation.1 | async-start | bytes 17301504 | tf_op jit(solution)/shard_map/all_gather | solution.py:58
  8.0 264.2 %all-reduce.3.cloned.1.call-start = ((), (), s32[]{:S(2)}) async-start(), calls=%async_computation.4 | async-start | bytes 1310720 | tf_op jit(solution)/shard_map/psum | solution.py:65
  195.9 3.3 copy-start
  195.9 224.5 %copy-start.1 = (f32[80]{0:T(128)S(1)}, f32[80]{0:T(128)}, u32[]{:S(2)}) copy-start(f32[80]{0:T(128)} %param.9) | copy-start | bytes 964
  208.3 231.8 %all-gather.9.cloned.1.call-start = ((), (), s32[]{:S(2)}) async-start(), calls=%async_computation.5 | async-start | bytes 21626880 | tf_op jit(solution)/shard_map/all_gather | solution.py:11
  272.2 209.3 %reduce-scatter.2.cloned.1.call-start = ((), (), s32[]{:S(2)}) async-start(), calls=%async_computation.3 | async-start | bytes 4718592 | tf_op jit(solution)/shard_map/reduce_scatter | solution.py:64
Sparse Core Ops, SparseCore 0:
  9.2 30.7 all-gather.6
  42.5 140.4 all-gather.4
  208.4 63.7 all-reduce.2
  274.6 161.0 all-gather.8
  440.2 35.2 reduce-scatter.1
where the time goes:
time: 492 us; the launch traced here: 491 us
  waiting for transfers between devices  236 us (48%)
  blocking collectives  148 us (30%)
  matrix products  43.8 us (9%)
  other arithmetic  42.5 us (9%)
  between operations  13.9 us (3%)
  local copies, waits for them, and re-layouts  4.96 us (1%)
    unnamed x1, blocking collectives  148 us
    all_gather x1, waiting for transfers between devices, per_device(): lax.all_gather(filter_mats, 'ctx', axis=1, tiled=True)  143 us
    psum x1, waiting for transfers between devices, per_device(): pole_sum = lax.psum(stacked[length:], 'grp')  63.9 us
    select_n x32, other arithmetic, step(): return jax.tree.map(lambda a, b: jnp.where(reached, a, b), new, before)  39.8 us
    all_gather x1, waiting for transfers between devices, per_device(): full_grad = lax.all_gather(out_grad, 'grp', axis=1, tiled=True)  27.7 us
    dot_general x1, matrix products, per_device(): jnp.einsum('kts,kti->si', kernel_mat, proj_grad, precision=exact_prec)  17.5 us
    dot_general x1, matrix products, per_device(): jnp.einsum('tj,kij->kti', full_grad, lax.all_gather(filter_mats, 'ctx', a...  12.9 us
  transfers between devices with their start and end apart: 5, of which 3 were waited for; matrix products, arithmetic and copies ran while one was open for 13% of the time, Pallas kernels for 0%

commit v1 on v0

--- a/solution.py
+++ b/solution.py
@@ -31,7 +31,14 @@
 
 
 def per_device(out_grad, filter_mats, coeffs, pole_rates):
-    full_grad = lax.all_gather(out_grad, "grp", axis=1, tiled=True)
+    size = lax.axis_size("grp")
+    right = [(i, (i + 1) % size) for i in range(size)]
+    blocks = [out_grad]
+    for far in range(1, size):
+        blocks = [lax.ppermute(blocks[0], "grp", right), *blocks]
+    whole = jnp.concatenate(blocks, axis=1)
+    turn = (lax.axis_index("grp") + 1) * blocks[-1].shape[1]
+    full_grad = jnp.roll(whole, turn, axis=1)
     length = full_grad.shape[0]
     col_width = out_grad.shape[1]
     poles = pole_rates.shape[0]

time: 492 us -> 457 us (0.929)
  waiting for transfers between devices: 236 us -> 192 us
  local copies, waits for them, and re-layouts: 4.96 us -> 17 us
    all_gather x1, waiting for transfers between devices: 143 us -> 82.2 us  [per_device(): lax.all_gather(filter_mats, 'ctx', axis=1, tiled=True)]
    ppermute x0 -> x7, waiting for transfers between devices: none -> 45.1 us  [per_device(): blocks = [lax.ppermute(blocks[0], 'grp', right), *blocks]]
    all_gather x1 -> x0, waiting for transfers between devices: 27.7 us -> none  [per_device(): full_grad = lax.all_gather(out_grad, 'grp', axis=1, tiled=True)]
    unnamed x6 -> x23, local copies, waits for them, and re-layouts: 4.53 us -> 15.8 us
  transfers between devices with their start and end apart: 5 -> 11, of which waited for: 3 -> 9; matrix products, arithmetic and copies ran while one was open for 13% -> 17% of each run, Pallas kernels for 0% -> 0%
where the time goes in v1:
time: 457 us; the launch traced here: 455 us
  waiting for transfers between devices  192 us (42%)
  blocking collectives  148 us (32%)
  other arithmetic  42.5 us (9%)
  matrix products  40.3 us (9%)
  local copies, waits for them, and re-layouts  17 us (4%)
  between operations  13.9 us (3%)
    unnamed x1, blocking collectives  148 us
    all_gather x1, waiting for transfers between devices, per_device(): lax.all_gather(filter_mats, 'ctx', axis=1, tiled=True)  82.2 us
    psum x1, waiting for transfers between devices, per_device(): pole_sum = lax.psum(stacked[length:], 'grp')  63.9 us
    ppermute x7, waiting for transfers between devices, per_device(): blocks = [lax.ppermute(blocks[0], 'grp', right), *blocks]  45.1 us
    select_n x32, other arithmetic, step(): return jax.tree.map(lambda a, b: jnp.where(reached, a, b), new, before)  39.8 us
    dot_general x1, matrix products, per_device(): jnp.einsum('kts,kti->si', kernel_mat, proj_grad, precision=exact_prec)  17.5 us
    unnamed x23, local copies, waits for them, and re-layouts  15.8 us
    dot_general x1, matrix products, per_device(): jnp.einsum('tj,kij->kti', full_grad, lax.all_gather(filter_mats, 'ctx', a...  12.4 us
  transfers between devices with their start and end apart: 11, of which 9 were waited for; matrix products, arithmetic and copies ran while one was open for 17% of the time, Pallas kernels for 0%

profile of v1, /device:TPU:0, one launch (start us, length us, event | category | flops | bytes accessed | tf_op | source)
XLA Modules:
  0.0 454.8 jit_solution(15140991876417399688)
XLA Ops:
  7.3 7.2 %collective-permute-done = bf16[512,256]{1,0:T(8,128)(2,1)S(1)} collective-permute-done((bf16[512,256]{1,0:T(8,128)(2,1)}, bf16[512,256]{1,0:T(8,128)(2,1)S(1)}, u32[]{:S(2)}, u32[]{:S(2)}) %collective-permute-start) | collective-permute-done | bytes 262176 | tf_op jit(solution)/shard_map/ppermute | solution.py:38
  14.5 7.0 %collective-permute-done.1 = bf16[512,256]{1,0:T(8,128)(2,1)S(1)} collective-permute-done((bf16[512,256]{1,0:T(8,128)(2,1)S(1)}, bf16[512,256]{1,0:T(8,128)(2,1)S(1)}, u32[]{:S(2)}, u32[]{:S(2)}) %collective-permute-start.1) | collective-permute-done | bytes 262176 | tf_op jit(solution)/shard_map/ppermute | solution.py:38
  21.5 7.0 %collective-permute-done.2 = bf16[512,256]{1,0:T(8,128)(2,1)S(1)} collective-permute-done((bf16[512,256]{1,0:T(8,128)(2,1)S(1)}, bf16[512,256]{1,0:T(8,128)(2,1)S(1)}, u32[]{:S(2)}, u32[]{:S(2)}) %collective-permute-start.2) | collective-permute-done | bytes 262176 | tf_op jit(solution)/shard_map/ppermute | solution.py:38
  28.6 7.0 %collective-permute-done.3 = bf16[512,256]{1,0:T(8,128)(2,1)S(1)} collective-permute-done((bf16[512,256]{1,0:T(8,128)(2,1)S(1)}, bf16[512,256]{1,0:T(8,128)(2,1)S(1)}, u32[]{:S(2)}, u32[]{:S(2)}) %collective-permute-start.3) | collective-permute-done | bytes 262176 | tf_op jit(solution)/shard_map/ppermute | solution.py:38
  35.6 1.3 dynamic-slice
  37.5 5.1 %collective-permute-done.4 = bf16[512,256]{1,0:T(8,128)(2,1)S(1)} collective-permute-done((bf16[512,256]{1,0:T(8,128)(2,1)S(1)}, bf16[512,256]{1,0:T(8,128)(2,1)S(1)}, u32[]{:S(2)}, u32[]{:S(2)}) %collective-permute-start.4) | collective-permute-done | bytes 262176 | tf_op jit(solution)/shard_map/ppermute | solution.py:38
  44.0 5.6 %collective-permute-done.5 = bf16[512,256]{1,0:T(8,128)(2,1)S(1)} collective-permute-done((bf16[512,256]{1,0:T(8,128)(2,1)S(1)}, bf16[512,256]{1,0:T(8,128)(2,1)S(1)}, u32[]{:S(2)}, u32[]{:S(2)}) %collective-permute-start.5) | collective-permute-done | bytes 262176 | tf_op jit(solution)/shard_map/ppermute | solution.py:38
  50.4 6.2 %collective-permute-done.6 = bf16[512,256]{1,0:T(8,128)(2,1)S(1)} collective-permute-done((bf16[512,256]{1,0:T(8,128)(2,1)S(1)}, bf16[512,256]{1,0:T(8,128)(2,1)S(1)}, u32[]{:S(2)}, u32[]{:S(2)}) %collective-permute-start.6) | collective-permute-done | bytes 262176 | tf_op jit(solution)/shard_map/ppermute | solution.py:38
  68.6 82.2 %all-gather.4.cloned.1.call-done = bf16[2,2048,2048]{2,1,0:T(8,128)(2,1)} async-done(((bf16[2,64,2048]{2,1,0:T(8,128)(2,1)}), bf16[2,2048,2048]{2,1,0:T(8,128)(2,1)}) %all-gather.4.cloned.1.call-update) | async-done | bytes 16777232 | tf_op jit(solution)/shard_map/all_gather | solution.py:65
  150.9 12.4 %fusion.11 = f32[512,2,2048]{2,0,1:T(8,128)S(1)} fusion(bf16[2,2048,2048]{2,1,0:T(8,128)(2,1)} %all-gather.4.cloned.1.call-done, bf16[512,4096]{1,0:T(8,128)(2,1)} %constant_dynamic-update-slice_fusion, s32[]{:T(128)S(6)} %select_n.59), kind=kOutput, calls=%fused_computation.9 | convolution fusion | flops 8589934592 | bytes 27262980 | tf_op jit(solution)/shard_map/tj,kij->kti/dot_general | solution.py:62
  163.3 3.3 copy-done
  166.5 6.0 %fusion.8 = f32[1,80,2048]{2,1,0:T(8,128)} fusion(f32[512,2,2048]{2,0,1:T(8,128)S(1)} %fusion.11, f32[80,512]{1,0:T(8,128)S(1)} %multiply_exponential_fusion, f32[2,80]{1,0:T(2,128)S(1)} %get-tuple-element.167), kind=kOutput, calls=%fused_computation.8 | convolution fusion | flops 2013347840 | bytes 9208448 | tf_op jit(solution)/shard_map/kpt,kti->pi/dot_general | solution.py:69
  172.6 63.9 %all-reduce.3.cloned.1.call-done = f32[1,80,2048]{2,1,0:T(8,128)} async-done(((f32[1,80,2048]{2,1,0:T(8,128)}), f32[1,80,2048]{2,1,0:T(8,128)}) %all-reduce.3.cloned.1.call-update) | async-done | bytes 655376 | tf_op jit(solution)/shard_map/psum | solution.py:72
  236.7 147.6 %all-reduce = f32[2560]{0:T(1024)S(1)} all-reduce(f32[2560]{0:T(1024)S(1)} %get-tuple-element.168), channel_id=2, replica_groups=mesh['ctx'=32,'grp'=8] {'ctx'}, use_global_device_ids=true, to_apply=%add | all-reduce | flops 2560 | bytes 20480
  384.9 1.9 fusion.18
  386.9 17.5 %fusion.5 = f32[512,2048]{1,0:T(8,128)} fusion(f32[512,2,2048]{2,0,1:T(8,128)} %copy-done, f32[2,512,512]{1,2,0:T(8,128)S(1)} %fusion.18, pred[512,512]{0,1:T(8,128)(4,1)S(1)} %iota_compare_fusion), kind=kOutput, calls=%fused_computation.7 | convolution fusion | flops 12885426176 | bytes 14942208 | tf_op jit(solution)/shard_map/kts,kti->si/dot_general | solution.py:68
  404.4 41.4 %while.16 = (s32[]{:T(128)}, f32[80,2048]{1,0:T(8,128)S(1)}, s32[]{:T(128)}, f32[32,80,2048]{2,1,0:T(8,128)}, f32[32,80,1]{1,2,0:T(1,128)S(1)}, /*index=5*/s32[]{:T(128)}, s32[]{:T(128)}, s32[]{:T(128)}, s32[]{:T(128)}) while((s32[]{:T(128)}, f32[80,2048]{1,0:T(8,128)S(1)}, s32[]{:T(128)}, f32[32,80,2048]{2,1,0:T(8,128)}, ...), condition=%wide.region_3.4_spmd.clone, body=%wide.region_2.3_spmd.clone.sunk | while | flops 655368 | bytes 1967207 | solution.py:24
  410.9 1.3 fusion.41
  414.8 1.2 fusion.41
  416.1 1.3 fusion.41
  417.4 1.2 fusion.41
  418.7 1.2 fusion.41
  420.0 1.2 fusion.41
  422.6 1.2 fusion.41
  423.9 1.2 fusion.41
  425.2 1.3 fusion.41
  426.5 1.3 fusion.41
  430.4 1.3 fusion.41
  431.7 1.3 fusion.41
  433.0 1.2 fusion.41
  439.4 1.2 fusion.41
  445.9 2.5 fusion.15
  (102 shorter events, 38.4 us)
Async XLA Ops:
  6.5 55.3 %copy-start.1 = (bf16[512,256]{1,0:T(8,128)(2,1)S(1)}, bf16[512,256]{1,0:T(8,128)(2,1)}, u32[]{:S(2)}) copy-start(bf16[512,256]{1,0:T(8,128)(2,1)} %param.6) | copy-start | bytes 786436
  6.5 144.3 %all-gather.4.cloned.1.call-start = ((), (), s32[]{:S(2)}) async-start(), calls=%async_computation.1 | async-start | bytes 17301504 | tf_op jit(solution)/shard_map/all_gather | solution.py:65
  7.3 229.3 %all-reduce.3.cloned.1.call-start = ((), (), s32[]{:S(2)}) async-start(), calls=%async_computation.3 | async-start | bytes 1310720 | tf_op jit(solution)/shard_map/psum | solution.py:72
  7.3 7.2 %collective-permute-start = (bf16[512,256]{1,0:T(8,128)(2,1)}, bf16[512,256]{1,0:T(8,128)(2,1)S(1)}, u32[]{:S(2)}, u32[]{:S(2)}) collective-permute-start(bf16[512,256]{1,0:T(8,128)(2,1)} %param.6), channel_id=1, source_target_pairs={{0,1},{1,2},{2,3},{3,4},{4,5},{5,6},{6,7},{7,0},{8,9},{9,10},{10,1... | collective-permute-start | bytes 786440 | tf_op jit(solution)/shard_map/ppermute | solution.py:38
  14.5 7.0 %collective-permute-start.1 = (bf16[512,256]{1,0:T(8,128)(2,1)S(1)}, bf16[512,256]{1,0:T(8,128)(2,1)S(1)}, u32[]{:S(2)}, u32[]{:S(2)}) collective-permute-start(bf16[512,256]{1,0:T(8,128)(2,1)S(1)} %collective-permute-done), channel_id=1, source_target_pairs={{0,1},{1,2},{2,3},{3,4},{4,5},{5,6},{6,7},{7,0},{8,9},{9,10},{10,1... | collective-permute-start | bytes 786440 | tf_op jit(solution)/shard_map/ppermute | solution.py:38
  21.5 7.0 %collective-permute-start.2 = (bf16[512,256]{1,0:T(8,128)(2,1)S(1)}, bf16[512,256]{1,0:T(8,128)(2,1)S(1)}, u32[]{:S(2)}, u32[]{:S(2)}) collective-permute-start(bf16[512,256]{1,0:T(8,128)(2,1)S(1)} %collective-permute-done.1), channel_id=1, source_target_pairs={{0,1},{1,2},{2,3},{3,4},{4,5},{5,6},{6,7},{7,0},{8,9},{9,10},{10,1... | collective-permute-start | bytes 786440 | tf_op jit(solution)/shard_map/ppermute | solution.py:38
  28.6 7.0 %collective-permute-start.3 = (bf16[512,256]{1,0:T(8,128)(2,1)S(1)}, bf16[512,256]{1,0:T(8,128)(2,1)S(1)}, u32[]{:S(2)}, u32[]{:S(2)}) collective-permute-start(bf16[512,256]{1,0:T(8,128)(2,1)S(1)} %collective-permute-done.2), channel_id=1, source_target_pairs={{0,1},{1,2},{2,3},{3,4},{4,5},{5,6},{6,7},{7,0},{8,9},{9,10},{10,1... | collective-permute-start | bytes 786440 | tf_op jit(solution)/shard_map/ppermute | solution.py:38
  35.6 7.0 %collective-permute-start.4 = (bf16[512,256]{1,0:T(8,128)(2,1)S(1)}, bf16[512,256]{1,0:T(8,128)(2,1)S(1)}, u32[]{:S(2)}, u32[]{:S(2)}) collective-permute-start(bf16[512,256]{1,0:T(8,128)(2,1)S(1)} %collective-permute-done.3), channel_id=1, source_target_pairs={{0,1},{1,2},{2,3},{3,4},{4,5},{5,6},{6,7},{7,0},{8,9},{9,10},{10,1... | collective-permute-start | bytes 786440 | tf_op jit(solution)/shard_map/ppermute | solution.py:38
  42.6 7.0 %collective-permute-start.5 = (bf16[512,256]{1,0:T(8,128)(2,1)S(1)}, bf16[512,256]{1,0:T(8,128)(2,1)S(1)}, u32[]{:S(2)}, u32[]{:S(2)}) collective-permute-start(bf16[512,256]{1,0:T(8,128)(2,1)S(1)} %collective-permute-done.4), channel_id=1, source_target_pairs={{0,1},{1,2},{2,3},{3,4},{4,5},{5,6},{6,7},{7,0},{8,9},{9,10},{10,1... | collective-permute-start | bytes 786440 | tf_op jit(solution)/shard_map/ppermute | solution.py:38
  49.6 7.0 %collective-permute-start.6 = (bf16[512,256]{1,0:T(8,128)(2,1)S(1)}, bf16[512,256]{1,0:T(8,128)(2,1)S(1)}, u32[]{:S(2)}, u32[]{:S(2)}) collective-permute-start(bf16[512,256]{1,0:T(8,128)(2,1)S(1)} %collective-permute-done.5), channel_id=1, source_target_pairs={{0,1},{1,2},{2,3},{3,4},{4,5},{5,6},{6,7},{7,0},{8,9},{9,10},{10,1... | collective-permute-start | bytes 786440 | tf_op jit(solution)/shard_map/ppermute | solution.py:38
  163.3 3.3 copy-start
  166.5 218.1 %copy-start.2 = (f32[80]{0:T(128)S(1)}, f32[80]{0:T(128)}, u32[]{:S(2)}) copy-start(f32[80]{0:T(128)} %param.9) | copy-start | bytes 964
  172.6 231.8 %all-gather.6.cloned.1.call-start = ((), (), s32[]{:S(2)}) async-start(), calls=%async_computation.4 | async-start | bytes 21626880 | tf_op jit(solution)/shard_map/all_gather | solution.py:11
  236.5 209.3 %reduce-scatter.2.cloned.1.call-start = ((), (), s32[]{:S(2)}) async-start(), calls=%async_computation.2 | async-start | bytes 4718592 | tf_op jit(solution)/shard_map/reduce_scatter | solution.py:71
Sparse Core Ops, SparseCore 0:
  9.9 140.8 all-gather.3
  172.7 63.7 all-reduce.2
  239.1 161.0 all-gather.5
  404.5 35.4 reduce-scatter.1
